TPU v7x, 32 devices: a whole 2x2x4 slice. The times are simulated.
32 devices in a mesh: ctx: 16 (over z, y, x), tp: 2 (over core).
Axes of the slice: x: 2, y: 2, z: 4, core: 2. Of those that a mesh axis runs over, the one named last changes fastest.
Arguments:
- queries: bfloat16 [2048, 4096], P('ctx', 'tp'), may hold values from -220 to 220
- keys: bfloat16 [2048, 1024], P('ctx', 'tp'), may hold values from -6 to 6
- values: bfloat16 [2048, 1024], P('ctx', 'tp'), may hold values from -6 to 6
- out_weight: bfloat16 [4096, 4096], P('tp'), may hold values from -0.09375 to 0.09375
- residual: bfloat16 [2048, 4096], P('ctx', 'tp'), may hold values from -1.5 to 1.5
- norm_gain: bfloat16 [4096], P('tp'), may hold values from 0.5 to 1.5
- span_order: int32 [32], replicated, may hold values from 0 to 31, as said below
Outputs:
- normed: bfloat16 [2048, 4096], P('ctx', 'tp')
Inputs may be any that keep to these rules, and one draw needn't show every extreme that they name: `span_order`: every span appears in exactly one slot. The two slots of one index d of ctx (slots 2d and 2d + 1) hold a span p and its mirror, the span at the same place counted from the end of the sequence; which index holds which pair, and the order of the two, are drawn.
All inputs are finite; a program needn't handle non-finite values.
Results may differ from a plain program's by a relative error of at most 0.009.
Values may be sent and summed in bfloat16 or wider, within the bound.
A program may use at most 64 MiB of HBM per device.

v0:
```python
import math

import jax
import jax.numpy as jnp
from jax import lax
from jax.sharding import PartitionSpec as P

D = 4096
HEAD_SIZE = 128


EPSILON = 1e-05


def per_device(queries, keys, values, out_weight, residual, norm_gain, span_order):
    local_rows = queries.shape[0]
    span_rows = local_rows // 2
    heads = queries.shape[1] // HEAD_SIZE
    kv_heads = keys.shape[1] // HEAD_SIZE
    group_size = heads // kv_heads
    scale = 1.0 / math.sqrt(HEAD_SIZE)
    device = lax.axis_index("ctx")
    owned = lax.dynamic_slice_in_dim(span_order, 2 * device, 2)
    offsets = jnp.arange(span_rows, dtype=jnp.int32)
    query_pos = (owned[:, None] * span_rows + offsets[None, :]).reshape(local_rows)
    query_mat = queries.reshape(local_rows, kv_heads, group_size, HEAD_SIZE)
    fresh = (
        jnp.full((kv_heads, group_size, local_rows), -1e30, jnp.float32),
        jnp.zeros((kv_heads, group_size, local_rows), jnp.float32),
        jnp.zeros((kv_heads, group_size, local_rows, HEAD_SIZE), jnp.float32),
    )
    carry = fresh
    key_piece = lax.all_gather(keys, "ctx", axis=0, tiled=True)
    value_piece = lax.all_gather(values, "ctx", axis=0, tiled=True)
    count = key_piece.shape[0]
    spans = count // span_rows
    per_step = max(1, min(spans, 1024 // span_rows))
    while spans % per_step != 0:
        per_step = per_step - 1
    steps = spans // per_step
    block_rows = per_step * span_rows
    key_pos_all = (span_order[:, None] * span_rows + offsets[None, :]).reshape(steps, block_rows)
    key_blocks = key_piece.reshape(steps, block_rows, kv_heads, HEAD_SIZE)
    value_blocks = value_piece.reshape(steps, block_rows, kv_heads, HEAD_SIZE)

    def scan_step(state, item):
        running, total, accum = state
        key_pos, key_mat, value_mat = item
        scores = (
            jnp.einsum("qhgd,khd->hgqk", query_mat, key_mat, preferred_element_type=jnp.float32)
            * scale
        )
        allowed = (key_pos[None, :] <= query_pos[:, None])[None, None, :, :]
        scores = jnp.where(allowed, scores, -1e30)
        newmax = jnp.maximum(running, jnp.max(scores, axis=-1))
        weights = jnp.where(allowed, jnp.exp(scores - newmax[..., None]), 0.0)
        fade = jnp.exp(running - newmax)
        total = total * fade + jnp.sum(weights, axis=-1)
        accum = accum * fade[..., None] + jnp.einsum(
            "hgqk,khd->hgqd",
            weights.astype(jnp.bfloat16),
            value_mat,
            preferred_element_type=jnp.float32,
        )
        return ((newmax, total, accum), None)

    carry, unused = lax.scan(scan_step, carry, (key_pos_all, key_blocks, value_blocks))
    running, total, accum = carry
    attended = accum / total[..., None]
    attended = (
        jnp.transpose(attended, (2, 0, 1, 3))
        .reshape(local_rows, heads * HEAD_SIZE)
        .astype(jnp.bfloat16)
    )
    partial_value = jnp.dot(attended, out_weight, preferred_element_type=jnp.float32)
    share = lax.psum_scatter(
        partial_value.astype(jnp.bfloat16), "tp", scatter_dimension=1, tiled=True
    ).astype(jnp.float32)
    hidden = (residual.astype(jnp.float32) + share).astype(jnp.bfloat16)
    hidden_f = hidden.astype(jnp.float32)
    squares = lax.psum(jnp.sum(hidden_f * hidden_f, axis=1), "tp")
    factor = lax.rsqrt(squares / D + EPSILON)
    normed = hidden_f * factor[:, None] * norm_gain.astype(jnp.float32)[None, :]
    return normed.astype(jnp.bfloat16)


def solution(mesh):
    return jax.shard_map(
        per_device,
        mesh=mesh,
        in_specs=(
            P("ctx", "tp"),
            P("ctx", "tp"),
            P("ctx", "tp"),
            P("tp", None),
            P("ctx", "tp"),
            P("tp"),
            P(),
        ),
        out_specs=P("ctx", "tp"),
        check_vma=False,
    )
```

profile of v0, /device:TPU:1, one launch (start us, length us, event | category | flops | bytes accessed | tf_op | source)
XLA Modules:
  0.0 205.8 jit_solution(13089571367657228611)
XLA Ops:
  6.5 0.7 all-gather.3.cloned.1.call-update
  7.3 0.7 all-gather.5.cloned.1.call-update
  8.1 1.3 copy.10
  9.4 1.0 copy.12
  10.4 0.7 broadcast_multiply_fusion
  11.4 0.7 dynamic-slice_multiply_fusion
  12.1 59.5 %all-gather.3.cloned.1.call-done = bf16[2048,512]{1,0:T(8,128)(2,1)} async-done(((bf16[128,512]{1,0:T(8,128)(2,1)}), bf16[2048,512]{1,0:T(8,128)(2,1)}) %all-gather.3.cloned.1.call-update) | async-done | bytes 2097168 | tf_op jit(solution)/shard_map/all_gather | solution.py:33
  71.6 2.5 %reshape.56 = bf16[2,1024,4,128]{3,2,1,0:T(4,128)(2,1)S(1)} reshape(bf16[2048,512]{1,0:T(8,128)(2,1)} %all-gather.3.cloned.1.call-done) | data formatting | bytes 4194304 | tf_op jit(solution)/shard_map/reshape | solution.py:43
  74.2 59.4 %all-gather.5.cloned.1.call-done = bf16[2048,512]{1,0:T(8,128)(2,1)} async-done(((bf16[128,512]{1,0:T(8,128)(2,1)}), bf16[2048,512]{1,0:T(8,128)(2,1)}) %all-gather.5.cloned.1.call-update) | async-done | bytes 2097168 | tf_op jit(solution)/shard_map/all_gather | solution.py:34
  133.6 4.0 %reshape.58 = bf16[2,1024,4,128]{3,2,1,0:T(4,128)(2,1)} reshape(bf16[2048,512]{1,0:T(8,128)(2,1)} %all-gather.5.cloned.1.call-done) | data formatting | bytes 4194304 | tf_op jit(solution)/shard_map/reshape | solution.py:44
  137.6 36.3 %while.15 = (s32[]{:T(128)}, f32[4,4,128]{2,1,0:T(4,128)S(1)}, f32[4,4,128]{2,1,0:T(4,128)S(1)}, f32[4,4,128,128]{3,2,1,0:T(8,128)}, s32[2,1024]{1,0:T(2,128)S(1...) while((s32[]{:T(128)}, f32[4,4,128]{2,1,0:T(4,128)S(1)}, ...), condition=%wide.region_3.4_spmd.clone, body=%wide.region_0.3_spmd.clone.sunk | while | flops 1101932672 | bytes 68303016 | solution.py:67
  137.7 0.1 le.33
  137.8 0.2 broadcast_compare_fusion.2
  138.0 2.0 constant_dynamic-slice_fusion.6
  140.0 5.6 %fusion.30 = (f32[4,4,128]{2,1,0:T(4,128)S(1)}, f32[4,1024,128,4]{2,1,3,0:T(8,128)}) fusion(pred[128,1024]{0,1:T(8,128)(4,1)S(1)} %broadcast_compare_fusion.2, bf16[128,4,4,128]{3,0,2,1:T(8,128)(2,1)} %get-tuple-element.216, bf16[1,1024,4,128]{3,2,1,0:T(4,128)(2,1)S(1)} %get-tuple-element.182), kind=kOutput, calls=%fused_computation.3.clone.1 | convolution fusion | flops 543160320 | bytes 10100736 | tf_op jit(solution)/shard_map/while/body/eval_jaxpr/qhgd,khd->hgqk/dot_general | solution.py:50
  145.6 4.6 %fusion.31 = f32[4,4,128]{2,1,0:T(4,128)S(1)} fusion(f32[4,1024,128,4]{2,1,3,0:T(8,128)} %get-tuple-element.184, f32[4,4,128]{2,1,0:T(4,128)S(1)} %select_maximum_fusion.2, pred[128,1024]{0,1:T(8,128)(4,1)S(1)} %broadcast_compare_fusion.2), kind=kLoop, calls=%fused_computation.5.clone.1 | loop fusion | flops 10483712 | bytes 8536064 | tf_op jit(solution)/shard_map/while/body/eval_jaxpr/reduce_sum | solution.py:58
  150.3 1.2 copy-done
  151.4 3.8 %fusion.33 = f32[4,4,128,128]{3,2,1,0:T(8,128)} fusion(f32[4,1024,128,4]{2,1,3,0:T(8,128)S(1)} %copy-done, f32[4,4,128]{2,1,0:T(4,128)S(1)} %select_maximum_fusion.2, pred[128,1024]{0,1:T(8,128)(4,1)S(1)} %broadcast_compare_fusion.2, bf16[1,1024,4,128]{3,2,1,0:T(4,128)(2,1)S(1)} %get-tuple-element.186, f32[4,4,128,128]{3,2,1,0:T(8,128)} %get-tuple-element.202, ...), kind=kOutput, calls=%fused_computation.8.clone.1 | convolution fusion | flops 548143104 | bytes 11681793 | tf_op jit(solution)/shard_map/while/body/eval_jaxpr/hgqk,khd->hgqd/dot_general | solution.py:59
  155.3 0.1 le.33
  155.4 0.2 broadcast_compare_fusion.2
  155.6 2.0 constant_dynamic-slice_fusion.6
  157.6 5.6 %fusion.30 = (f32[4,4,128]{2,1,0:T(4,128)S(1)}, f32[4,1024,128,4]{2,1,3,0:T(8,128)}) fusion(pred[128,1024]{0,1:T(8,128)(4,1)S(1)} %broadcast_compare_fusion.2, bf16[128,4,4,128]{3,0,2,1:T(8,128)(2,1)} %get-tuple-element.216, bf16[1,1024,4,128]{3,2,1,0:T(4,128)(2,1)S(1)} %get-tuple-element.182), kind=kOutput, calls=%fused_computation.3.clone.1 | convolution fusion | flops 543160320 | bytes 10100736 | tf_op jit(solution)/shard_map/while/body/eval_jaxpr/qhgd,khd->hgqk/dot_general | solution.py:50
  163.2 4.6 %fusion.31 = f32[4,4,128]{2,1,0:T(4,128)S(1)} fusion(f32[4,1024,128,4]{2,1,3,0:T(8,128)} %get-tuple-element.184, f32[4,4,128]{2,1,0:T(4,128)S(1)} %select_maximum_fusion.2, pred[128,1024]{0,1:T(8,128)(4,1)S(1)} %broadcast_compare_fusion.2), kind=kLoop, calls=%fused_computation.5.clone.1 | loop fusion | flops 10483712 | bytes 8536064 | tf_op jit(solution)/shard_map/while/body/eval_jaxpr/reduce_sum | solution.py:58
  167.9 1.2 copy-done
  169.1 4.8 %fusion.33 = f32[4,4,128,128]{3,2,1,0:T(8,128)} fusion(f32[4,1024,128,4]{2,1,3,0:T(8,128)S(1)} %copy-done, f32[4,4,128]{2,1,0:T(4,128)S(1)} %select_maximum_fusion.2, pred[128,1024]{0,1:T(8,128)(4,1)S(1)} %broadcast_compare_fusion.2, bf16[1,1024,4,128]{3,2,1,0:T(4,128)(2,1)S(1)} %get-tuple-element.186, f32[4,4,128,128]{3,2,1,0:T(8,128)} %get-tuple-element.202, ...), kind=kOutput, calls=%fused_computation.8.clone.1 | convolution fusion | flops 548143104 | bytes 11681793 | tf_op jit(solution)/shard_map/while/body/eval_jaxpr/hgqk,khd->hgqd/dot_general | solution.py:59
  173.9 1.6 copy.14
  175.4 0.1 divide_convert_fusion
  175.6 9.2 %convolution_convert_fusion = bf16[128,4096]{1,0:T(8,128)(2,1)} fusion(bf16[128,2048]{0,1:T(8,128)(2,1)S(1)} %bitcast.49, bf16[2048,4096]{1,0:T(8,128)(2,1)} %param.12), kind=kOutput, calls=%fused_computation.25 | convolution fusion | flops 2148007936 | bytes 18350080 | tf_op jit(solution)/shard_map/dot_general | solution.py:75
  184.8 8.6 %reduce-scatter.2.cloned.1.call-done = bf16[128,2048]{1,0:T(8,128)(2,1)} async-done(((bf16[128,4096]{1,0:T(8,128)(2,1)}), bf16[128,2048]{1,0:T(8,128)(2,1)}) %reduce-scatter.2.cloned.1.call-update) | async-done | bytes 524304 | tf_op jit(solution)/shard_map/reduce_scatter | solution.py:76
  193.5 1.3 fusion.16
  194.8 2.5 %psum.7 = f32[128]{0:T(128)S(1)} all-reduce(f32[128]{0:T(128)S(1)} %fusion.16), channel_id=1, replica_groups=mesh['ctx'=16,'tp'=2] {'tp'}, use_global_device_ids=true, to_apply=%region_6.7 | all-reduce | flops 128 | bytes 1024 | tf_op jit(solution)/shard_map/psum | solution.py:81
  197.3 2.0 fusion.18
  (31 shorter events, 0.7 us)
Async XLA Ops:
  6.5 65.1 %all-gather.3.cloned.1.call-start = ((), (), s32[]{:S(2)}) async-start(), calls=%async_computation.1 | async-start | bytes 2228224 | tf_op jit(solution)/shard_map/all_gather | solution.py:33
  7.3 126.4 %all-gather.5.cloned.1.call-start = ((), (), s32[]{:S(2)}) async-start(), calls=%async_computation.2 | async-start | bytes 2228224 | tf_op jit(solution)/shard_map/all_gather | solution.py:34
  8.0 185.5 %reduce-scatter.2.cloned.1.call-start = ((), (), s32[]{:S(2)}) async-start(), calls=%async_computation.3 | async-start | bytes 1572864 | tf_op jit(solution)/shard_map/reduce_scatter | solution.py:76
  145.6 5.8 %copy-start = (f32[4,1024,128,4]{2,1,3,0:T(8,128)S(1)}, f32[4,1024,128,4]{2,1,3,0:T(8,128)}, u32[]{:S(2)}) copy-start(f32[4,1024,128,4]{2,1,3,0:T(8,128)} %get-tuple-element.184) | copy-start | bytes 25165828 | tf_op jit(solution)/shard_map/while
  163.2 5.8 %copy-start = (f32[4,1024,128,4]{2,1,3,0:T(8,128)S(1)}, f32[4,1024,128,4]{2,1,3,0:T(8,128)}, u32[]{:S(2)}) copy-start(f32[4,1024,128,4]{2,1,3,0:T(8,128)} %get-tuple-element.184) | copy-start | bytes 25165828 | tf_op jit(solution)/shard_map/while
  175.6 9.2 %copy-start.2 = (bf16[2048]{0:T(1024)(128)(2,1)S(1)}, bf16[2048]{0:T(1024)(128)(2,1)}, u32[]{:S(2)}) copy-start(bf16[2048]{0:T(1024)(128)(2,1)} %param.14) | copy-start | bytes 12292
  175.6 17.9 %copy-start.1 = (bf16[128,2048]{1,0:T(8,128)(2,1)S(1)}, bf16[128,2048]{1,0:T(8,128)(2,1)}, u32[]{:S(2)}) copy-start(bf16[128,2048]{1,0:T(8,128)(2,1)} %param.13) | copy-start | bytes 1572868
Sparse Core Ops, SparseCore 0:
  10.1 61.4 all-gather.2
  74.4 59.1 all-gather.4
  184.9 8.4 reduce-scatter.1
where the time goes:
time: 207 us; the launch traced here: 206 us
  waiting for transfers between devices  129 us (62%)
  matrix products  29.1 us (14%)
  local copies, waits for them, and re-layouts  17.2 us (8%)
  other arithmetic  14.7 us (7%)
  between operations  13.2 us (6%)
  blocking collectives  2.47 us (1%)
    all_gather x1, waiting for transfers between devices, per_device(): key_piece = lax.all_gather(keys, 'ctx', axis=0, tiled=True)  59.5 us
    all_gather x1, waiting for transfers between devices, per_device(): value_piece = lax.all_gather(values, 'ctx', axis=0, tiled=True)  59.4 us
    dot_general x2, matrix products, scan_step(): jnp.einsum('qhgd,khd->hgqk', query_mat, key_mat, preferred_element_type=j...  11.3 us
    reduce_sum x2, other arithmetic, scan_step(): total = total * fade + jnp.sum(weights, axis=-1)  9.21 us
    dot_general x1, matrix products, per_device(): jnp.dot(attended, out_weight, preferred_element_type=jnp.float32)  9.19 us
    reduce_scatter x1, waiting for transfers between devices, per_device(): lax.psum_scatter(partial_value.astype(jnp.bfloat16), 'tp', scatter_dimens...  8.64 us
    dot_general x2, matrix products, scan_step(): jnp.einsum('hgqk,khd->hgqd', weights.astype(jnp.bfloat16), value_mat, pre...  8.61 us
  transfers between devices with their start and end apart: 3, of which 3 were waited for; matrix products, arithmetic and copies ran while one was open for 3% of the time, Pallas kernels for 0%

commit v1 on v0

v1 whole, which is shorter than its diff:
```python
import functools
import math

import jax
import jax.numpy as jnp
from jax import lax
from jax.experimental import pallas as pl
from jax.experimental.pallas import tpu as pltpu
from jax.sharding import PartitionSpec as P

HEAD_SIZE = 128
EPSILON = 1e-05
MESH = pl.DeviceIdType.MESH
GROUP = 4


def factor(n):
    bits = n.bit_length() - 1
    if n != 1 << bits:
        return (n, 1, 1)
    inner = bits // 3
    return (1 << (bits - 2 * inner), 1 << inner, 1 << inner)


def pick(index, table):
    value = jnp.int32(table[-1])
    for i in range(len(table) - 1):
        value = jnp.where(index == i, jnp.int32(table[i]), value)
    return value


def nearest(n):
    return [sorted(range(n), key=lambda s: (abs(s - c), s)) for c in range(n)]


def rank_order(sizes, weights):
    ranks = [
        (a, b, c)
        for a in range(sizes[0])
        for b in range(sizes[1])
        for c in range(sizes[2])
    ]
    return sorted(ranks, key=lambda r: (sum(x * w for x, w in zip(r, weights)), r[::-1]))


def kernel(
    n_ctx, n_tp, span_ref, q_hbm, k_hbm, v_hbm, w_hbm, res_hbm, gain_hbm, out_ref,
    kv, q, q_t, bias, acc, top, total, att, w, res, gain, sendbuf, recvbuf, hid, sq_out, sq_in,
    local_sem, send_sem, recv_sem, rs_send, rs_recv, sq_send, sq_recv,
):
    rows = q_hbm.shape[0]
    span_rows = rows // 2
    kv_heads = k_hbm.shape[1] // HEAD_SIZE
    heads = q_hbm.shape[1] // HEAD_SIZE
    group = heads // kv_heads
    lanes = group * rows
    features = res_hbm.shape[1]
    scale2 = math.log2(math.e) / math.sqrt(HEAD_SIZE)
    sizes = factor(n_ctx)
    me = lax.axis_index("ctx")
    tp = lax.axis_index("tp")

    cz = me // (sizes[1] * sizes[2])
    cy = (me // sizes[2]) % sizes[1]
    cx = me % sizes[2]
    odd = tp % 2
    if sizes[1] == sizes[2]:
        ca = cy + odd * (cx - cy)
        cb = cx + odd * (cy - cx)
        sa = sizes[2] + odd * (1 - sizes[2])
        sb = 1 + odd * (sizes[2] - 1)
    else:
        ca, cb, sa, sb = cy, cx, sizes[2], 1
    coords = (cz, ca, cb)
    strides = (sizes[1] * sizes[2], sa, sb)
    near = []
    for d in range(3):
        table = nearest(sizes[d])
        near.append([pick(coords[d], [table[c][r] for c in range(sizes[d])]) for r in range(sizes[d])])

    def neighbours(d):
        n, c, s = sizes[d], coords[d], strides[d]
        if n == 1:
            return []
        if n == 2:
            return [(None, me + (1 - 2 * c) * s)]
        return [(c < n - 1, me + s), (c > 0, me - s)]

    def when(valid, body):
        if valid is None:
            body()
        else:
            pl.when(valid)(body)

    loads = []
    for h in range(kv_heads):
        cols = pl.ds(h * HEAD_SIZE, HEAD_SIZE)
        loads.append(pltpu.make_async_copy(k_hbm.at[:, cols], kv.at[me, h, 0], local_sem.at[2 * h]))
        loads.append(pltpu.make_async_copy(v_hbm.at[:, cols], kv.at[me, h, 1], local_sem.at[2 * h + 1]))
    load_q = pltpu.make_async_copy(q_hbm, q, local_sem.at[2 * kv_heads])
    load_w = pltpu.make_async_copy(w_hbm, w, local_sem.at[2 * kv_heads + 1])
    load_r = pltpu.make_async_copy(res_hbm, res, local_sem.at[2 * kv_heads + 2])
    load_g = pltpu.make_async_copy(gain_hbm, gain, local_sem.at[2 * kv_heads + 3])
    for copy in loads:
        copy.start()
    load_q.start()

    barrier = pltpu.get_barrier_semaphore()
    expected = jnp.int32(n_tp - 1)
    for d in range(3):
        for valid, device in neighbours(d):
            def greet(device=device):
                pl.semaphore_signal(barrier, inc=1, device_id={"ctx": device}, device_id_type=MESH)
            when(valid, greet)
            expected = expected + (1 if valid is None else valid.astype(jnp.int32))
    for j in range(1, n_tp):
        pl.semaphore_signal(barrier, inc=1, device_id={"tp": lax.rem(tp + j, n_tp)}, device_id_type=MESH)
    pl.semaphore_wait(barrier, expected)

    sends = []

    def send(h, src, valid, device):
        slot = len(sends)
        copy = pltpu.make_async_remote_copy(
            src_ref=kv.at[src, h],
            dst_ref=kv.at[src, h],
            send_sem=send_sem.at[slot],
            recv_sem=recv_sem.at[h, src],
            device_id={"ctx": device},
            device_id_type=MESH,
        )
        when(valid, copy.start)
        sends.append((valid, copy))

    last_first = kv_heads // 4
    orders, walks = [], []
    for h in range(kv_heads):
        if h < kv_heads - last_first:
            order, weights = (0, 1, 2), (1.0, 1.1, 2.2)
        else:
            order, weights = (1, 2, 0), (1.0, 1.1, 3.0)
        orders.append(order)
        walks.append(rank_order([sizes[d] for d in order], weights))

    def source(h, ranks):
        src = jnp.int32(0)
        for d, r in zip(orders[h], ranks):
            src = src + near[d][r] * strides[d]
        return src

    def arrive(h, ranks):
        order = orders[h]
        src = source(h, ranks)
        moved = [k for k in range(3) if ranks[k] > 0]
        last = moved[-1] if moved else -1
        if moved:
            pltpu.make_async_copy(kv.at[src, h], kv.at[src, h], recv_sem.at[h, src]).wait()
            d = order[last]
            if sizes[d] > 2:
                c, s = coords[d], near[d][ranks[last]]
                up = (s < c).astype(jnp.int32)
                step = 2 * up - 1
                ahead = c + step
                send(h, src, jnp.logical_and(ahead >= 0, ahead < sizes[d]), me + step * strides[d])
        for k in range(last + 1, 3):
            for valid, device in neighbours(order[k]):
                send(h, src, valid, device)
        return src

    for h in range(kv_heads):
        loads[2 * h].wait()
        loads[2 * h + 1].wait()
        arrive(h, (0, 0, 0))
    load_w.start()
    load_r.start()
    load_g.start()

    row = lax.broadcasted_iota(jnp.int32, (rows, rows), 0)
    lane = lax.broadcasted_iota(jnp.int32, (rows, rows), 1)

    def position(index, device):
        first, second = span_ref[2 * device], span_ref[2 * device + 1]
        return index + jnp.where(index < span_rows, first * span_rows, (second - 1) * span_rows)

    query_pos = position(lane, me)

    @pl.loop(0, n_ctx)
    def _(src):
        bias[src] = jnp.where(position(row, src) <= query_pos, 0.0, -1e30)

    load_q.wait()
    for h in range(heads):
        q_t[h // group, :, (h % group) * rows:(h % group + 1) * rows] = (
            q[:, h * HEAD_SIZE:(h + 1) * HEAD_SIZE].T
        )

    width = min(lanes, 256)

    def attend(h, srcs, first):
        v_t = jnp.concatenate([kv[s, h, 1].T for s in srcs], axis=1)
        keys = [kv[s, h, 0] for s in srcs]
        masks = [jnp.concatenate([bias[s]] * (width // rows), axis=1) for s in srcs]
        for at in range(0, lanes, width):
            cols = pl.ds(at, width)
            qq = q_t[h, :, cols]
            scores = jnp.concatenate(
                [jnp.dot(k, qq, preferred_element_type=jnp.float32) + m for k, m in zip(keys, masks)], axis=0
            )
            new = jnp.max(scores, axis=0, keepdims=True)
            if not first:
                old = top[h, :, cols]
                new = jnp.maximum(old, new)
            weights = jnp.exp2((scores - new) * scale2)
            part = jnp.sum(weights, axis=0, keepdims=True)
            value = jnp.dot(v_t, weights.astype(jnp.bfloat16), preferred_element_type=jnp.float32)
            if not first:
                fade = jnp.exp2((old - new) * scale2)
                part = part + total[h, :, cols] * fade
                value = value + acc[h, :, cols] * fade
            top[h, :, cols] = new
            total[h, :, cols] = part
            acc[h, :, cols] = value

    pending = [[(0, 0, 0)] for _ in range(kv_heads)]
    for p in range(1, n_ctx):
        for h in range(kv_heads):
            arrive(h, walks[h][p])
            pending[h].append(walks[h][p])
            if len(pending[h]) == GROUP or p == n_ctx - 1:
                attend(h, [source(h, r) for r in pending[h]], p < GROUP)
                pending[h] = []

    for h in range(heads):
        cols = pl.ds((h % group) * rows, rows)
        done = acc[h // group, :, cols] / total[h // group, :, cols]
        att[:, h * HEAD_SIZE:(h + 1) * HEAD_SIZE] = done.astype(jnp.bfloat16).T

    chunk = min(features, 512)
    chunks = features // chunk
    load_w.wait()
    att_all = att[...]

    def project(owner, c):
        cols = pl.ds(pl.multiple_of(owner * features + c * chunk, chunk), chunk)
        return jnp.dot(att_all, w[:, cols], preferred_element_type=jnp.float32)

    shares = []
    for j in range(1, n_tp):
        peer = lax.rem(tp + j, n_tp)
        for c in range(chunks):
            sendbuf[j - 1, c] = project(peer, c).astype(jnp.bfloat16)
            copy = pltpu.make_async_remote_copy(
                src_ref=sendbuf.at[j - 1, c],
                dst_ref=recvbuf.at[j - 1, c],
                send_sem=rs_send.at[j - 1, c],
                recv_sem=rs_recv.at[j - 1, c],
                device_id={"tp": peer},
                device_id_type=MESH,
            )
            copy.start()
            shares.append(copy)
    load_r.wait()
    own = [project(tp, c) for c in range(chunks)]
    squares = jnp.zeros((rows, HEAD_SIZE), jnp.float32)
    for c in range(chunks):
        share = own[c]
        for j in range(1, n_tp):
            shares[(j - 1) * chunks + c].wait_recv()
            share = share + recvbuf[j - 1, c].astype(jnp.float32)
        cols = slice(c * chunk, (c + 1) * chunk)
        hidden = (res[:, cols].astype(jnp.float32) + share).astype(jnp.bfloat16)
        hid[:, cols] = hidden
        hidden = hidden.astype(jnp.float32)
        for i in range(0, chunk, HEAD_SIZE):
            piece = hidden[:, i:i + HEAD_SIZE]
            squares = squares + piece * piece
    mine = jnp.sum(squares.T, axis=0, keepdims=True)
    sq_out[...] = jnp.broadcast_to(mine, sq_out.shape)
    last = []
    for j in range(1, n_tp):
        copy = pltpu.make_async_remote_copy(
            src_ref=sq_out,
            dst_ref=sq_in.at[j - 1],
            send_sem=sq_send.at[j - 1],
            recv_sem=sq_recv.at[j - 1],
            device_id={"tp": lax.rem(tp + j, n_tp)},
            device_id_type=MESH,
        )
        copy.start()
        last.append(copy)
    load_g.wait()
    for valid, copy in sends:
        when(valid, copy.wait_send)
    for copy in shares:
        copy.wait_send()
    for j, copy in enumerate(last):
        copy.wait_recv()
        mine = mine + sq_in[j][0:1]
    inverse = lax.rsqrt(mine / (features * n_tp) + EPSILON)
    inverse = jnp.broadcast_to(inverse, (HEAD_SIZE, rows)).T
    for i in range(0, features, HEAD_SIZE):
        cols = slice(i, i + HEAD_SIZE)
        normed = hid[:, cols].astype(jnp.float32) * inverse * gain[:, cols].astype(jnp.float32)
        out_ref[:, cols] = normed.astype(jnp.bfloat16)
    for copy in last:
        copy.wait_send()


def per_device(n_ctx, n_tp, queries, keys, values, out_weight, residual, norm_gain, span_order):
    rows = queries.shape[0]
    heads = queries.shape[1] // HEAD_SIZE
    kv_heads = keys.shape[1] // HEAD_SIZE
    lanes = heads // kv_heads * rows
    features = residual.shape[1]
    chunk = min(features, 512)
    chunks = features // chunk
    peers = max(1, n_tp - 1)
    bf, f32 = jnp.bfloat16, jnp.float32
    hbm = pl.BlockSpec(memory_space=pl.ANY)
    vmem = pltpu.VMEM
    dma = pltpu.SemaphoreType.DMA
    return pl.pallas_call(
        functools.partial(kernel, n_ctx, n_tp),
        out_shape=jax.ShapeDtypeStruct((rows, features), bf),
        in_specs=[pl.BlockSpec(memory_space=pltpu.SMEM)] + [hbm] * 6,
        out_specs=pl.BlockSpec(memory_space=pltpu.VMEM),
        scratch_shapes=[
            vmem((n_ctx, kv_heads, 2, rows, HEAD_SIZE), bf),
            vmem((rows, heads * HEAD_SIZE), bf),
            vmem((kv_heads, HEAD_SIZE, lanes), bf),
            vmem((n_ctx, rows, rows), f32),
            vmem((kv_heads, HEAD_SIZE, lanes), f32),
            vmem((kv_heads, 1, lanes), f32),
            vmem((kv_heads, 1, lanes), f32),
            vmem((rows, heads * HEAD_SIZE), bf),
            vmem(out_weight.shape, bf),
            vmem((rows, features), bf),
            vmem((1, features), bf),
            vmem((peers, chunks, rows, chunk), bf),
            vmem((peers, chunks, rows, chunk), bf),
            vmem((rows, features), bf),
            vmem((8, rows), f32),
            vmem((peers, 8, rows), f32),
            dma((2 * kv_heads + 4,)),
            dma((kv_heads * 6 * n_ctx // 2,)),
            dma((kv_heads, n_ctx)),
            dma((peers, chunks)),
            dma((peers, chunks)),
            dma((peers,)),
            dma((peers,)),
        ],
        compiler_params=pltpu.CompilerParams(
            collective_id=0, has_side_effects=True, vmem_limit_bytes=60 * 1024 * 1024
        ),
    )(span_order, queries, keys, values, out_weight, residual, norm_gain.reshape(1, features))


def solution(mesh):
    return jax.shard_map(
        functools.partial(per_device, mesh.shape["ctx"], mesh.shape["tp"]),
        mesh=mesh,
        in_specs=(
            P("ctx", "tp"),
            P("ctx", "tp"),
            P("ctx", "tp"),
            P("tp", None),
            P("ctx", "tp"),
            P("tp"),
            P(),
        ),
        out_specs=P("ctx", "tp"),
        check_vma=False,
    )
```

time: 207 us -> 51.3 us (0.25)
  waiting for transfers between devices: 129 us -> 0 us
  Pallas kernels: 0 us -> 47.9 us
  matrix products: 29.1 us -> 0 us
  other arithmetic: 14.7 us -> 0 us
  local copies, waits for them, and re-layouts: 17.2 us -> 3.17 us
  between operations: 13.2 us -> 0.01 us
  blocking collectives: 2.47 us -> 0 us
    all_gather x2 -> x0, waiting for transfers between devices: 119 us -> none  [the longest x1 59.5 us: per_device(): key_piece = lax.all_gather(keys, 'ctx', axis=0, tiled=True)]
    pallas_call x0 -> x1, Pallas kernels: none -> 47.9 us  [per_device(): pl.pallas_call(functools.partial(kernel, n_ctx, n_tp), out_shape=jax.Shap...]
    dot_general x5 -> x0, matrix products: 29.1 us -> none  [the longest x2 11.3 us: scan_step(): jnp.einsum('qhgd,khd->hgqk', query_mat, key_mat, preferred_element_type=j...]
    reduce_sum x3 -> x0, other arithmetic: 10.5 us -> none  [the longest x2 9.21 us: scan_step(): total = total * fade + jnp.sum(weights, axis=-1)]
    reduce_scatter x1 -> x0, waiting for transfers between devices: 8.64 us -> none  [per_device(): lax.psum_scatter(partial_value.astype(jnp.bfloat16), 'tp', scatter_dimens...]
    reshape x2 -> x1, local copies, waits for them, and re-layouts: 6.54 us -> 1.29 us  [per_device(): norm_gain.reshape(1, features)]
    while x7 -> x0, local copies, waits for them, and re-layouts: 3.95 us -> none
    dynamic_slice x4 -> x0, local copies, waits for them, and re-layouts: 3.92 us -> none  [per_device(): lax.scan(scan_step, carry, (key_pos_all, key_blocks, value_blocks))]
  transfers between devices with their start and end apart: 3 -> 0, of which waited for: 3 -> 0; matrix products, arithmetic and copies ran while one was open for 3% -> 0% of each run, Pallas kernels for 0% -> 0%
where the time goes in v1:
time: 51.3 us; the launch traced here: 51.1 us
  Pallas kernels  47.9 us (93%)
  local copies, waits for them, and re-layouts  3.17 us (6%)
    pallas_call x1, Pallas kernels, per_device(): pl.pallas_call(functools.partial(kernel, n_ctx, n_tp), out_shape=jax.Shap...  47.9 us
    unnamed x1, local copies, waits for them, and re-layouts  1.88 us
    reshape x1, local copies, waits for them, and re-layouts, per_device(): norm_gain.reshape(1, features)  1.29 us

profile of v1, /device:TPU:1, one launch (start us, length us, event | category | flops | bytes accessed | tf_op | source)
XLA Modules:
  0.0 51.1 jit_solution(11075840307362133792)
XLA Ops:
  0.0 1.3 %reshape.3.gain_hbm = bf16[1,2048]{1,0:T(2,128)(2,1)} reshape(bf16[2048]{0:T(1024)(128)(2,1)} %param.12) | data formatting | bytes 8192 | tf_op jit(solution)/shard_map/reshape | solution.py:355
  1.3 47.9 %shard_map.73 = bf16[128,2048]{1,0:T(8,128)(2,1)} custom-call(s32[32]{0:T(128)} %span_ref.1, bf16[128,2048]{1,0:T(8,128)(2,1)} %q_hbm.1, bf16[128,512]{1,0:T(8,128)(2,1)} %k_hbm.1, bf16[128,512]{1,0:T(8,128)(2,1)} %v_hbm.1, bf16[2048,4096]{1,0:T(8,128)(2,1)} %w_hbm.1, bf16[128,2048]{1,0:T(8,128)(2,1)} %res_hbm.1, bf16[1,2048]{1,0:T(2,128)(2,1)} %reshape.3.gain_hbm), custom_call_target="tpu_custom_call" | custom-call | tf_op jit(solution)/shard_map/pallas_call | solution.py:322
  49.2 1.9 %copy.9 = bf16[128,2048]{1,0:T(8,128)(2,1)} copy(bf16[128,2048]{1,0:T(8,128)(2,1)} %shard_map.73) | data formatting | bytes 1048576

commit v2 on v1

--- a/solution.py
+++ b/solution.py
@@ -101,9 +101,6 @@
     load_w = pltpu.make_async_copy(w_hbm, w, local_sem.at[2 * kv_heads + 1])
     load_r = pltpu.make_async_copy(res_hbm, res, local_sem.at[2 * kv_heads + 2])
     load_g = pltpu.make_async_copy(gain_hbm, gain, local_sem.at[2 * kv_heads + 3])
-    for copy in loads:
-        copy.start()
-    load_q.start()
 
     barrier = pltpu.get_barrier_semaphore()
     expected = jnp.int32(n_tp - 1)
@@ -115,6 +112,9 @@
             expected = expected + (1 if valid is None else valid.astype(jnp.int32))
     for j in range(1, n_tp):
         pl.semaphore_signal(barrier, inc=1, device_id={"tp": lax.rem(tp + j, n_tp)}, device_id_type=MESH)
+    for copy in loads:
+        copy.start()
+    load_q.start()
     pl.semaphore_wait(barrier, expected)
 
     sends = []
@@ -300,7 +300,7 @@
     inverse = jnp.broadcast_to(inverse, (HEAD_SIZE, rows)).T
     for i in range(0, features, HEAD_SIZE):
         cols = slice(i, i + HEAD_SIZE)
-        normed = hid[:, cols].astype(jnp.float32) * inverse * gain[:, cols].astype(jnp.float32)
+        normed = hid[:, cols].astype(jnp.float32) * inverse * gain[cols].astype(jnp.float32)[None, :]
         out_ref[:, cols] = normed.astype(jnp.bfloat16)
     for copy in last:
         copy.wait_send()
@@ -335,7 +335,7 @@
             vmem((rows, heads * HEAD_SIZE), bf),
             vmem(out_weight.shape, bf),
             vmem((rows, features), bf),
-            vmem((1, features), bf),
+            vmem((features,), bf),
             vmem((peers, chunks, rows, chunk), bf),
             vmem((peers, chunks, rows, chunk), bf),
             vmem((rows, features), bf),
@@ -352,7 +352,7 @@
         compiler_params=pltpu.CompilerParams(
             collective_id=0, has_side_effects=True, vmem_limit_bytes=60 * 1024 * 1024
         ),
-    )(span_order, queries, keys, values, out_weight, residual, norm_gain.reshape(1, features))
+    )(span_order, queries, keys, values, out_weight, residual, norm_gain)
 
 
 def solution(mesh):

time: 51.3 us -> 50 us (0.975)
  local copies, waits for them, and re-layouts: 3.17 us -> 1.88 us
    reshape x1 -> x0, local copies, waits for them, and re-layouts: 1.29 us -> none  [per_device(): norm_gain.reshape(1, features)]
where the time goes in v2:
time: 50 us; the launch traced here: 49.8 us
  Pallas kernels  47.9 us (96%)
  local copies, waits for them, and re-layouts  1.88 us (4%)
    pallas_call x1, Pallas kernels, per_device(): pl.pallas_call(functools.partial(kernel, n_ctx, n_tp), out_shape=jax.Shap...  47.9 us
    unnamed x1, local copies, waits for them, and re-layouts  1.88 us

profile of v2, /device:TPU:1, one launch (start us, length us, event | category | flops | bytes accessed | tf_op | source)
XLA Modules:
  0.0 49.8 jit_solution(13361803249589449094)
XLA Ops:
  0.0 47.9 %shard_map.73 = bf16[128,2048]{1,0:T(8,128)(2,1)} custom-call(s32[32]{0:T(128)} %span_ref.1, bf16[128,2048]{1,0:T(8,128)(2,1)} %q_hbm.1, bf16[128,512]{1,0:T(8,128)(2,1)} %k_hbm.1, bf16[128,512]{1,0:T(8,128)(2,1)} %v_hbm.1, bf16[2048,4096]{1,0:T(8,128)(2,1)} %w_hbm.1, bf16[128,2048]{1,0:T(8,128)(2,1)} %res_hbm.1, bf16[2048]{0:T(1024)(128)(2,1)} %gain_hbm.1), custom_call_target="tpu_custom_call" | custom-call | tf_op jit(solution)/shard_map/pallas_call | solution.py:322
  47.9 1.9 %copy.9 = bf16[128,2048]{1,0:T(8,128)(2,1)} copy(bf16[128,2048]{1,0:T(8,128)(2,1)} %shard_map.73) | data formatting | bytes 1048576

commit v3 on v2

--- a/solution.py
+++ b/solution.py
@@ -226,8 +226,8 @@
         for h in range(kv_heads):
             arrive(h, walks[h][p])
             pending[h].append(walks[h][p])
-            if len(pending[h]) == GROUP or p == n_ctx - 1:
-                attend(h, [source(h, r) for r in pending[h]], p < GROUP)
+            if len(pending[h]) == GROUP or p in (n_ctx - 3, n_ctx - 1):
+                attend(h, [source(h, r) for r in pending[h]], len(pending[h]) == p + 1)
                 pending[h] = []
 
     for h in range(heads):

time: 50 us -> 51.2 us (1.024)
  Pallas kernels: 47.9 us -> 48.8 us
    pallas_call x1, Pallas kernels: 47.9 us -> 48.8 us  [per_device(): pl.pallas_call(functools.partial(kernel, n_ctx, n_tp), out_shape=jax.Shap...]
where the time goes in v3:
time: 51.2 us; the launch traced here: 50.7 us
  Pallas kernels  48.8 us (95%)
  local copies, waits for them, and re-layouts  1.88 us (4%)
    pallas_call x1, Pallas kernels, per_device(): pl.pallas_call(functools.partial(kernel, n_ctx, n_tp), out_shape=jax.Shap...  48.8 us
    unnamed x1, local copies, waits for them, and re-layouts  1.88 us

profile of v3, /device:TPU:1, one launch (start us, length us, event | category | flops | bytes accessed | tf_op | source)
XLA Modules:
  0.0 50.7 jit_solution(12169195038563390706)
XLA Ops:
  0.0 48.8 %shard_map.73 = bf16[128,2048]{1,0:T(8,128)(2,1)} custom-call(s32[32]{0:T(128)} %span_ref.1, bf16[128,2048]{1,0:T(8,128)(2,1)} %q_hbm.1, bf16[128,512]{1,0:T(8,128)(2,1)} %k_hbm.1, bf16[128,512]{1,0:T(8,128)(2,1)} %v_hbm.1, bf16[2048,4096]{1,0:T(8,128)(2,1)} %w_hbm.1, bf16[128,2048]{1,0:T(8,128)(2,1)} %res_hbm.1, bf16[2048]{0:T(1024)(128)(2,1)} %gain_hbm.1), custom_call_target="tpu_custom_call" | custom-call | tf_op jit(solution)/shard_map/pallas_call | solution.py:322
  48.8 1.9 %copy.9 = bf16[128,2048]{1,0:T(8,128)(2,1)} copy(bf16[128,2048]{1,0:T(8,128)(2,1)} %shard_map.73) | data formatting | bytes 1048576
